TPU v7x, 32 devices: a whole 2x2x4 slice. The times are simulated.
32 devices in a mesh: grp: 2 (over y), stn: 4 (over z), chan: 4 (over x, core).
Axes of the slice: x: 2, y: 2, z: 4, core: 2. Of those that a mesh axis runs over, the one named last changes fastest.
Arguments:
- voltages: bfloat16 [256, 31, 8192], P(('grp', 'stn', 'chan')), parts along dimension 0, may hold values from -6 to 6
- taps: float32 [16, 8192], replicated, may hold values from -1.5 to 1.5
Outputs:
- visibilities: bfloat16 [8, 3, 256, 2, 1024], P(('grp', 'stn'), None, 'chan'), parts along dimension 0
There are 2 independent parts, one for each index of `grp`. A program takes and returns all parts, laid end to end along the dimension named above; an argument that names none is the same for every part. Nothing has to cross between parts.
All inputs are finite; a program needn't handle non-finite values.
Results may differ from a plain program's by a relative error of at most 0.0053.
Values may be sent and summed in bfloat16 or wider, within the bound.
No kernel may reach another device: no remote copies, remote signals or barrier semaphores. Data moves between devices by JAX's collectives and lax.ppermute only.
A program may use at most 64 MiB of HBM per device.

v0:
```python
import functools
import math

import jax
import jax.numpy as jnp
import numpy as np
from jax import lax
from jax.experimental import pallas as pl
from jax.experimental.pallas import tpu as pltpu
from jax.sharding import PartitionSpec as P

AVG = 16
LANES = 128
SUB = 8
f32 = jnp.float32
bf16 = jnp.bfloat16


def add(a, b):
    return b if a is None else a if b is None else a + b


def sub(a, b):
    if b is None:
        return a
    return -b if a is None else a - b


def turn(re, im, num, den):
    num %= den
    if num == 0:
        return re, im
    if 4 * num == den:
        return im, None if re is None else -re
    if 2 * num == den:
        return (None if re is None else -re), (None if im is None else -im)
    if 4 * num == 3 * den:
        return (None if im is None else -im), re
    c = math.cos(2 * math.pi * num / den)
    s = math.sin(2 * math.pi * num / den)
    if 8 * num == den or 8 * num == 5 * den:
        if im is None:
            return re * c, re * -s
        if re is None:
            return im * s, im * c
        return (re + im) * c, (im - re) * c
    if im is None:
        return re * c, re * -s
    if re is None:
        return im * s, im * c
    return re * c + im * s, im * c - re * s


def fft(values, needed):
    size = len(values)
    if size == 1:
        return values
    if all(im is None for _, im in values):
        half_need = size // 4 + 1 if size >= 4 else size // 2
        even = fft(values[0::2], min(half_need, size // 2))
        odd = fft(values[1::2], min(half_need, size // 2))

        def mirrored(part, k):
            n = size // 2
            if k < len(part):
                return part[k]
            re, im = part[n - k]
            return re, (None if im is None else -im)

        out = [None] * size
        for k in range(size // 2):
            if k >= needed and k + size // 2 >= needed:
                continue
            er, ei = mirrored(even, k)
            tr, ti = turn(*mirrored(odd, k), k, size)
            out[k] = (add(er, tr), add(ei, ti))
            out[k + size // 2] = (sub(er, tr), sub(ei, ti))
        return out[:needed]
    even = fft(values[0::2], size // 2)
    odd = fft(values[1::2], size // 2)
    out = [None] * size
    for k in range(size // 2):
        er, ei = even[k]
        tr, ti = turn(*odd[k], k, size)
        out[k] = (add(er, tr), add(ei, ti))
        out[k + size // 2] = (sub(er, tr), sub(ei, ti))
    return out[:needed]


def spectra_kernel(tw_ref, t_ref, x_ref, taps_ref, z_ref, xs_ref, w_ref, a_ref, f_ref, xp_ref, s_ref, *, sizes):
    inputs, frames, tiles, per_step, spectra_count, tap_count = sizes
    half = tiles // 2
    kept = LANES // 2
    rows = (half + 1) * spectra_count
    block = AVG * spectra_count
    parts = tiles // AVG
    step = pl.program_id(0)

    def one_tile(here, carry):
        lanes = pl.ds(pl.multiple_of(here * LANES, LANES), LANES)
        for one in range(inputs):
            xs_ref[pl.ds(one, frames, stride=SUB), :] = x_ref[one, :, lanes].astype(f32)
        weights = [jnp.broadcast_to(taps_ref[t : t + 1, lanes], (SUB, LANES)) for t in range(tap_count)]
        at = (step * per_step + here) * SUB
        for s in range(spectra_count):
            total = weights[0] * xs_ref[s * SUB : (s + 1) * SUB, :]
            for t in range(1, tap_count):
                total = total + weights[t] * xs_ref[(s + t) * SUB : (s + t + 1) * SUB, :]
            w_ref[pl.ds(pl.multiple_of(s * tiles * SUB + at, SUB), SUB), :] = total
        return carry

    lax.fori_loop(0, per_step, one_tile, 0)

    @pl.when(step == pl.num_programs(0) - 1)
    def finish():
        radix = 8
        other = tiles // radix
        columns = radix // 2 + 1

        def one_spectrum(s, carry):
            base = s * tiles * SUB
            present = {}
            for b in range(other):
                got = [
                    (w_ref[pl.ds(pl.multiple_of(base + (other * a + b) * SUB, SUB), SUB), :], None)
                    for a in range(radix)
                ]
                for ka, (re, im) in enumerate(fft(got, columns)):
                    if ka:
                        re, im = turn(re, im, ka * b, tiles)
                    for c, value in enumerate((re, im)):
                        present[ka, b, c] = value is not None
                        if value is not None:
                            at = ((ka * other + b) * 2 + c) * SUB
                            a_ref[at : at + SUB, :] = value
            for ka in range(columns):
                got = []
                for b in range(other):
                    at = (ka * other + b) * 2 * SUB
                    got.append(
                        tuple(
                            a_ref[at + c * SUB : at + (c + 1) * SUB, :] if present[ka, b, c] else None
                            for c in range(2)
                        )
                    )
                need = other if 0 < ka else other // 2 + 1
                done = fft(got, need)
                for kb, (re, im) in enumerate(done):
                    direct = ka + radix * kb
                    if direct <= half:
                        k1, conj = direct, False
                    else:
                        k1, conj = tiles - direct, True
                        if k1 % radix == ka:
                            continue
                    if im is None:
                        im = jnp.zeros_like(re)
                    if conj:
                        im = -im
                    cos = tw_ref[k1 * 2 * SUB : (k1 * 2 + 1) * SUB, :]
                    sin = tw_ref[(k1 * 2 + 1) * SUB : (k1 * 2 + 2) * SUB, :]
                    where = k1 * spectra_count + s
                    f_ref[pl.ds(where, SUB, stride=rows), :] = re * cos + im * sin
                    f_ref[pl.ds(SUB * rows + where, SUB, stride=rows), :] = im * cos - re * sin
            return carry

        lax.fori_loop(0, spectra_count, one_spectrum, 0)

        def one_input(one, carry):
            for c in range(2):
                value = f_ref[pl.ds(pl.multiple_of((c * SUB + one) * rows, SUB), rows), :]
                high = value.astype(bf16)
                xp_ref[:, c * LANES : (c + 1) * LANES] = high
                xp_ref[:, (2 + c) * LANES : (3 + c) * LANES] = (value - high.astype(f32)).astype(bf16)
            for j in range(parts):
                if j < parts // 2:
                    first = j * block
                    which = 0
                else:
                    first = ((parts - 1 - j) * AVG + 1) * spectra_count
                    which = 1
                right = xp_ref[first : first + block, :]
                dims = (((1,), (1,)), ((), ()))
                out = lax.dot_general(
                    t_ref[which, :, : 4 * LANES], right, dims, preferred_element_type=f32
                ) + lax.dot_general(
                    t_ref[which, :, 4 * LANES :], right[:, : 2 * LANES], dims, preferred_element_type=f32
                )
                for c in range(2):
                    for h in range(block // LANES):
                        tile = (j * 2 + c) * (block // LANES) + h
                        s_ref[pl.ds(tile * kept * SUB + one, kept, stride=SUB), :] = out[
                            c * kept : (c + 1) * kept, h * LANES : (h + 1) * LANES
                        ]
            return carry

        lax.fori_loop(0, inputs, one_input, 0)

        wide = 2 * block // LANES

        def one_row(m, carry):
            for j in range(parts):
                for tile in range(wide):
                    at = pl.multiple_of(((j * wide + tile) * kept + m) * SUB, SUB)
                    z_ref[m * parts + j, :, tile * LANES : (tile + 1) * LANES] = s_ref[
                        pl.ds(at, SUB), :
                    ][:inputs].astype(bf16)
            return carry

        lax.fori_loop(0, kept, one_row, 0)


def tables(frame_len):
    tiles = frame_len // LANES
    half = tiles // 2
    kept = LANES // 2
    k1 = np.arange(half + 1)[:, None]
    p = np.arange(LANES)[None, :]
    angle = 2 * np.pi * ((k1 * p) % frame_len) / frame_len
    tw = np.stack([np.cos(angle), np.sin(angle)], axis=1)[:, :, None, :]
    tw = np.broadcast_to(tw, (half + 1, 2, SUB, LANES)).reshape(-1, LANES).astype(np.float32)

    def one(m, sign):
        theta = 2 * np.pi * ((m[:, None] * p) % LANES) / LANES
        cos, sin = np.cos(theta), np.sin(theta)
        full = np.concatenate(
            [np.concatenate([cos, sin], axis=1), sign * np.concatenate([-sin, cos], axis=1)], axis=0
        )
        full = (full * frame_len ** (-0.5)).astype(np.float32)
        high = full.astype(jnp.bfloat16)
        low = (full - high.astype(np.float32)).astype(jnp.bfloat16)
        return np.concatenate([high, high, low], axis=1)

    m = np.arange(kept)
    return tw, np.stack([one(m, 1.0), one(LANES - 1 - m, -1.0)])


def make_spectra(voltages, taps):
    inputs, frames, frame_len = voltages.shape
    tap_count = taps.shape[0]
    spectra_count = frames - tap_count + 1
    tiles = frame_len // LANES
    half = tiles // 2
    rows = (half + 1) * spectra_count
    block = AVG * spectra_count
    groups = frame_len // 2 // AVG
    per_step = 8
    tw, t = tables(frame_len)
    sizes = (inputs, frames, tiles, per_step, spectra_count, tap_count)
    return pl.pallas_call(
        functools.partial(spectra_kernel, sizes=sizes),
        name="spectra",
        grid=(tiles // per_step,),
        in_specs=[
            pl.BlockSpec(tw.shape, lambda q: (0, 0)),
            pl.BlockSpec(t.shape, lambda q: (0, 0, 0)),
            pl.BlockSpec((inputs, frames, per_step * LANES), lambda q: (0, 0, q)),
            pl.BlockSpec((tap_count, per_step * LANES), lambda q: (0, q)),
        ],
        out_specs=pl.BlockSpec((groups, inputs, 2 * block), lambda q: (0, 0, 0)),
        out_shape=jax.ShapeDtypeStruct((groups, inputs, 2 * block), bf16),
        scratch_shapes=[
            pltpu.VMEM(((frames + 1) * SUB, LANES), f32),
            pltpu.VMEM((spectra_count * tiles * SUB, LANES), f32),
            pltpu.VMEM((5 * (tiles // 8) * 2 * SUB, LANES), f32),
            pltpu.VMEM((2 * SUB * rows, LANES), f32),
            pltpu.VMEM((rows, 4 * LANES), bf16),
            pltpu.VMEM((groups * (2 * block // LANES) * SUB, LANES), f32),
        ],
    )(jnp.asarray(tw), jnp.asarray(t), voltages, taps)


def correlate_kernel(r_ref, o_ref, left_ref, right_ref, p_ref, q_ref, *, sizes):
    stations, chans, inputs, reach, scale = sizes
    block_inputs = chans * inputs
    wide = r_ref.shape[-1]
    copies = LANES // block_inputs
    out_rows = block_inputs * block_inputs // LANES
    for b in range(stations):
        own = jnp.concatenate([r_ref[c * stations + b, 0] for c in range(chans)], axis=0)
        at = b * 2 * block_inputs
        left_ref[at : at + block_inputs, :] = own
        left_ref[at + block_inputs : at + 2 * block_inputs, : wide // 2] = own[:, wide // 2 :]
        left_ref[at + block_inputs : at + 2 * block_inputs, wide // 2 :] = -own[:, : wide // 2]
        for r in range(copies):
            right_ref[b * LANES + r * block_inputs : b * LANES + (r + 1) * block_inputs, :] = own
    place = lax.broadcasted_iota(jnp.int32, (out_rows, LANES), 1) // block_inputs

    def one_target(target, carry):
        right = right_ref[pl.ds(pl.multiple_of(target * LANES, LANES), LANES), :]
        for d in range(reach):
            b = lax.rem(target - d + stations, stations)
            left = left_ref[pl.ds(pl.multiple_of(b * 2 * block_inputs, 2 * block_inputs), 2 * block_inputs), :]
            out = lax.dot_general(left, right, (((1,), (1,)), ((), ())), preferred_element_type=f32)
            p_ref[d, :, :] = out * scale
            for part in range(2):
                value = p_ref[d, pl.ds(part * block_inputs, out_rows, stride=copies), :]
                for r in range(1, copies):
                    value = jnp.where(
                        place == r, p_ref[d, pl.ds(part * block_inputs + r, out_rows, stride=copies), :], value
                    )
                q_ref[d, pl.ds(part, out_rows, stride=2), :] = value
            o_ref[b, d, 0, :, :] = q_ref[d].astype(bf16)
        return carry

    lax.fori_loop(0, stations, one_target, 0)


def correlate(turned, stations, chans, reach, scale):
    sources, groups, inputs, wide = turned.shape
    block_inputs = chans * inputs
    out_rows = block_inputs * block_inputs // LANES
    sizes = (stations, chans, inputs, reach, scale)
    return pl.pallas_call(
        functools.partial(correlate_kernel, sizes=sizes),
        name="correlate",
        grid=(groups,),
        in_specs=[pl.BlockSpec((sources, 1, inputs, wide), lambda g: (0, g, 0, 0))],
        out_specs=pl.BlockSpec((stations, reach, 1, 2 * out_rows, LANES), lambda g: (0, 0, g, 0, 0)),
        out_shape=jax.ShapeDtypeStruct((stations, reach, groups, 2 * out_rows, LANES), bf16),
        scratch_shapes=[
            pltpu.VMEM((stations * 2 * block_inputs, wide), bf16),
            pltpu.VMEM((stations * LANES, wide), bf16),
            pltpu.VMEM((reach, 2 * block_inputs, LANES), f32),
            pltpu.VMEM((reach, 2 * out_rows, LANES), f32),
        ],
    )(turned)


def local(voltages, taps):
    inputs_here, frames, frame_len = voltages.shape
    spectra_count = frames - taps.shape[0] + 1
    stations = lax.axis_size("stn")
    chans = lax.axis_size("chan")
    reach = stations // 2 + 1
    block_inputs = chans * inputs_here
    pairs = block_inputs * block_inputs
    spectra = make_spectra(voltages, taps)
    groups, _, wide = spectra.shape
    here = groups // (stations * chans)
    send = spectra.reshape(chans * stations, here, inputs_here, wide)
    turned = lax.all_to_all(send, ("chan", "stn"), 0, 0, tiled=True)
    tiles = correlate(turned, stations, chans, reach, 1.0 / (spectra_count * AVG))
    back = lax.all_to_all(tiles, "stn", 0, 0, tiled=True)
    out = back.transpose(1, 0, 2, 3, 4).reshape(reach, stations * here, pairs // LANES, 2, LANES)
    out = out.transpose(0, 1, 3, 2, 4).reshape(1, reach, stations * here, 2, pairs)
    return out


def solution(mesh):
    placed = (P(("grp", "stn", "chan"), None, None), P())
    return jax.shard_map(
        local,
        mesh=mesh,
        in_specs=placed,
        out_specs=P(("grp", "stn"), None, "chan", None, None),
        check_vma=False,
    )
```

profile of v0, /device:TPU:0, one launch (start us, length us, event | category | flops | bytes accessed | tf_op | source)
XLA Modules:
  0.0 128.5 jit_solution(10479530756126738811)
XLA Ops:
  0.0 6.3 %copy.8.x_ref = bf16[8,31,8192]{2,1,0:T(8,128)(2,1)} copy(bf16[8,31,8192]{2,0,1:T(8,128)(2,1)} %param.4) | data formatting | bytes 8126464 | tf_op args[0]
  6.3 20.0 %spectra.1 = bf16[256,8,512]{2,1,0:T(8,128)(2,1)} custom-call(f32[528,128]{1,0:T(8,128)} %constant.4.clone.tw_ref, bf16[2,128,768]{2,1,0:T(8,128)(2,1)} %constant.5.clone.t_ref, bf16[8,31,8192]{2,1,0:T(8,128)(2,1)} %copy.8.x_ref, f32[16,8192]{1,0:T(8,128)} %taps_ref.1), custom_call_target="tpu_custom_call" | custom-call | tf_op jit(solution)/shard_map/spectra/pallas_call | solution.py:250
  26.3 56.8 %all_to_all.10.r_ref = bf16[16,16,8,512]{3,2,1,0:T(8,128)(2,1)} all-to-all(bf16[16,16,8,512]{3,2,1,0:T(8,128)(2,1)} %bitcast.7), channel_id=1, replica_groups=mesh['grp'=2,'stn'=4,'chan'=4] {'chan','stn'}, dimensions={0} | all-to-all | bytes 4194304 | tf_op jit(solution)/shard_map/all_to_all | solution.py:342
  83.1 19.8 %correlate.1 = bf16[4,3,16,16,128]{4,3,2,1,0:T(8,128)(2,1)} custom-call(bf16[16,16,8,512]{3,2,1,0:T(8,128)(2,1)} %all_to_all.10.r_ref), custom_call_target="tpu_custom_call" | custom-call | tf_op jit(solution)/shard_map/correlate/pallas_call | solution.py:314
  103.0 23.8 %all_to_all.11 = bf16[4,3,16,16,128]{4,3,2,1,0:T(8,128)(2,1)S(1)} all-to-all(bf16[4,3,16,16,128]{4,3,2,1,0:T(8,128)(2,1)} %correlate.1), channel_id=1, replica_groups=mesh['grp'=2,'stn'=4,'chan'=4] {'stn'}, dimensions={0} | all-to-all | bytes 1572864 | tf_op jit(solution)/shard_map/all_to_all | solution.py:344
  126.7 0.2 copy.9
  127.0 0.5 copy.12
  127.5 1.1 reshape.12
where the time goes:
time: 129 us
  blocking collectives  80.6 us (62%)
  Pallas kernels  39.9 us (31%)
  local copies, waits for them, and re-layouts  8.08 us (6%)
    all_to_all x1, blocking collectives, local(): turned = lax.all_to_all(send, ('chan', 'stn'), 0, 0, tiled=True)  56.8 us
    all_to_all x1, blocking collectives, local(): back = lax.all_to_all(tiles, 'stn', 0, 0, tiled=True)  23.8 us
    pallas_call x1, Pallas kernels, make_spectra(): pl.pallas_call(functools.partial(spectra_kernel, sizes=sizes), name='spec...  20 us
    pallas_call x1, Pallas kernels, correlate(): pl.pallas_call(functools.partial(correlate_kernel, sizes=sizes), name='co...  19.8 us
    unnamed x1, local copies, waits for them, and re-layouts  6.3 us

commit v1 on v0

--- a/solution.py
+++ b/solution.py
@@ -98,8 +98,8 @@
 
     def one_tile(here, carry):
         lanes = pl.ds(pl.multiple_of(here * LANES, LANES), LANES)
-        for one in range(inputs):
-            xs_ref[pl.ds(one, frames, stride=SUB), :] = x_ref[one, :, lanes].astype(f32)
+        for frame in range(frames):
+            xs_ref[frame * SUB : frame * SUB + inputs, :] = x_ref[frame, :, lanes].astype(f32)
         weights = [jnp.broadcast_to(taps_ref[t : t + 1, lanes], (SUB, LANES)) for t in range(tap_count)]
         at = (step * per_step + here) * SUB
         for s in range(spectra_count):
@@ -236,7 +236,7 @@
 
 
 def make_spectra(voltages, taps):
-    inputs, frames, frame_len = voltages.shape
+    frames, inputs, frame_len = voltages.shape
     tap_count = taps.shape[0]
     spectra_count = frames - tap_count + 1
     tiles = frame_len // LANES
@@ -254,7 +254,7 @@
         in_specs=[
             pl.BlockSpec(tw.shape, lambda q: (0, 0)),
             pl.BlockSpec(t.shape, lambda q: (0, 0, 0)),
-            pl.BlockSpec((inputs, frames, per_step * LANES), lambda q: (0, 0, q)),
+            pl.BlockSpec((frames, inputs, per_step * LANES), lambda q: (0, 0, q)),
             pl.BlockSpec((tap_count, per_step * LANES), lambda q: (0, q)),
         ],
         out_specs=pl.BlockSpec((groups, inputs, 2 * block), lambda q: (0, 0, 0)),
@@ -270,59 +270,69 @@
     )(jnp.asarray(tw), jnp.asarray(t), voltages, taps)
 
 
-def correlate_kernel(r_ref, o_ref, left_ref, right_ref, p_ref, q_ref, *, sizes):
-    stations, chans, inputs, reach, scale = sizes
+def correlate_kernel(r_ref, o_ref, p_ref, q_ref, *, sizes):
+    stations, chans, inputs, reach, scale, per_step = sizes
     block_inputs = chans * inputs
     wide = r_ref.shape[-1]
     copies = LANES // block_inputs
     out_rows = block_inputs * block_inputs // LANES
-    for b in range(stations):
-        own = jnp.concatenate([r_ref[c * stations + b, 0] for c in range(chans)], axis=0)
-        at = b * 2 * block_inputs
-        left_ref[at : at + block_inputs, :] = own
-        left_ref[at + block_inputs : at + 2 * block_inputs, : wide // 2] = own[:, wide // 2 :]
-        left_ref[at + block_inputs : at + 2 * block_inputs, wide // 2 :] = -own[:, : wide // 2]
-        for r in range(copies):
-            right_ref[b * LANES + r * block_inputs : b * LANES + (r + 1) * block_inputs, :] = own
     place = lax.broadcasted_iota(jnp.int32, (out_rows, LANES), 1) // block_inputs
 
-    def one_target(target, carry):
-        right = right_ref[pl.ds(pl.multiple_of(target * LANES, LANES), LANES), :]
+    def fetch(b, g):
+        return jnp.concatenate([r_ref[c * stations + b, g] for c in range(chans)], axis=0)
+
+    def lefts(own):
+        crossed = jnp.concatenate([own[:, wide // 2 :], -own[:, : wide // 2]], axis=1)
+        return [own, crossed]
+
+    def one_target(target, g, blocks, slot):
+        right = jnp.concatenate([blocks[0][0]] * copies, axis=0)
+        left = jnp.concatenate([piece for pair in blocks for piece in pair], axis=0)
+        out = lax.dot_general(left, right, (((1,), (1,)), ((), ())), preferred_element_type=f32)
+        p_ref[slot, :, :] = out * scale
         for d in range(reach):
-            b = lax.rem(target - d + stations, stations)
-            left = left_ref[pl.ds(pl.multiple_of(b * 2 * block_inputs, 2 * block_inputs), 2 * block_inputs), :]
-            out = lax.dot_general(left, right, (((1,), (1,)), ((), ())), preferred_element_type=f32)
-            p_ref[d, :, :] = out * scale
+            b = target - d
+            b = b % stations if isinstance(b, int) else lax.rem(b + stations, stations)
             for part in range(2):
-                value = p_ref[d, pl.ds(part * block_inputs, out_rows, stride=copies), :]
+                base = (2 * d + part) * block_inputs
+                value = p_ref[slot, pl.ds(base, out_rows, stride=copies), :]
                 for r in range(1, copies):
-                    value = jnp.where(
-                        place == r, p_ref[d, pl.ds(part * block_inputs + r, out_rows, stride=copies), :], value
-                    )
-                q_ref[d, pl.ds(part, out_rows, stride=2), :] = value
-            o_ref[b, d, 0, :, :] = q_ref[d].astype(bf16)
-        return carry
-
-    lax.fori_loop(0, stations, one_target, 0)
+                    value = jnp.where(place == r, p_ref[slot, pl.ds(base + r, out_rows, stride=copies), :], value)
+                q_ref[slot, d, pl.ds(part, out_rows, stride=2), :] = value
+            o_ref[b, d, g, :, :] = q_ref[slot, d].astype(bf16)
+
+    for g in range(per_step):
+        if stations <= 4:
+            pairs = [lefts(fetch(b, g)) for b in range(stations)]
+            for target in range(stations):
+                one_target(target, g, [pairs[target - d] for d in range(reach)], g * stations + target)
+        else:
+
+            def body(target, carry, g=g):
+                blocks = [lefts(fetch(lax.rem(target - d + stations, stations), g)) for d in range(reach)]
+                one_target(target, g, blocks, 0)
+                return carry
+
+            lax.fori_loop(0, stations, body, 0)
 
 
 def correlate(turned, stations, chans, reach, scale):
     sources, groups, inputs, wide = turned.shape
     block_inputs = chans * inputs
     out_rows = block_inputs * block_inputs // LANES
-    sizes = (stations, chans, inputs, reach, scale)
+    per_step = math.gcd(groups, 2)
+    sizes = (stations, chans, inputs, reach, scale, per_step)
+    slots = per_step * stations if stations <= 4 else 1
     return pl.pallas_call(
         functools.partial(correlate_kernel, sizes=sizes),
         name="correlate",
-        grid=(groups,),
-        in_specs=[pl.BlockSpec((sources, 1, inputs, wide), lambda g: (0, g, 0, 0))],
-        out_specs=pl.BlockSpec((stations, reach, 1, 2 * out_rows, LANES), lambda g: (0, 0, g, 0, 0)),
+        grid=(groups // per_step,),
+        in_specs=[pl.BlockSpec((sources, per_step, inputs, wide), lambda g: (0, g, 0, 0))],
+        out_specs=pl.BlockSpec((stations, reach, per_step, 2 * out_rows, LANES), lambda g: (0, 0, g, 0, 0)),
         out_shape=jax.ShapeDtypeStruct((stations, reach, groups, 2 * out_rows, LANES), bf16),
         scratch_shapes=[
-            pltpu.VMEM((stations * 2 * block_inputs, wide), bf16),
-            pltpu.VMEM((stations * LANES, wide), bf16),
-            pltpu.VMEM((reach, 2 * block_inputs, LANES), f32),
-            pltpu.VMEM((reach, 2 * out_rows, LANES), f32),
+            pltpu.VMEM((slots, reach * 2 * block_inputs, LANES), f32),
+            pltpu.VMEM((slots, reach, 2 * out_rows, LANES), f32),
         ],
     )(turned)
 
@@ -335,7 +345,7 @@
     reach = stations // 2 + 1
     block_inputs = chans * inputs_here
     pairs = block_inputs * block_inputs
-    spectra = make_spectra(voltages, taps)
+    spectra = make_spectra(voltages.transpose(1, 0, 2), taps)
     groups, _, wide = spectra.shape
     here = groups // (stations * chans)
     send = spectra.reshape(chans * stations, here, inputs_here, wide)

time: 129 us -> 110 us (0.85)
  Pallas kernels: 39.9 us -> 26.9 us
  local copies, waits for them, and re-layouts: 8.08 us -> 1.78 us
    pallas_call x1, Pallas kernels: 19.8 us -> 7.79 us  [correlate(): pl.pallas_call(functools.partial(correlate_kernel, sizes=sizes), name='co...]
    unnamed x1 -> x0, local copies, waits for them, and re-layouts: 6.3 us -> none
where the time goes in v1:
time: 110 us; the launch traced here: 109 us
  blocking collectives  80.6 us (73%)
  Pallas kernels  26.9 us (24%)
  local copies, waits for them, and re-layouts  1.78 us (2%)
    all_to_all x1, blocking collectives, local(): turned = lax.all_to_all(send, ('chan', 'stn'), 0, 0, tiled=True)  56.8 us
    all_to_all x1, blocking collectives, local(): back = lax.all_to_all(tiles, 'stn', 0, 0, tiled=True)  23.8 us
    pallas_call x1, Pallas kernels, make_spectra(): pl.pallas_call(functools.partial(spectra_kernel, sizes=sizes), name='spec...  19.1 us
    pallas_call x1, Pallas kernels, correlate(): pl.pallas_call(functools.partial(correlate_kernel, sizes=sizes), name='co...  7.79 us

profile of v1, /device:TPU:0, one launch (start us, length us, event | category | flops | bytes accessed | tf_op | source)
XLA Modules:
  0.0 109.3 jit_solution(14978454469167737146)
XLA Ops:
  0.0 19.1 %spectra.1 = bf16[256,8,512]{2,1,0:T(8,128)(2,1)} custom-call(f32[528,128]{1,0:T(8,128)} %constant.4.clone.tw_ref, bf16[2,128,768]{2,1,0:T(8,128)(2,1)} %constant.5.clone.t_ref, bf16[31,8,8192]{2,1,0:T(8,128)(2,1)} %bitcast.9, f32[16,8192]{1,0:T(8,128)} %taps_ref.1), custom_call_target="tpu_custom_call" | custom-call | tf_op jit(solution)/shard_map/spectra/pallas_call | solution.py:250
  19.1 56.8 %all_to_all.10.r_ref = bf16[16,16,8,512]{3,2,1,0:T(8,128)(2,1)} all-to-all(bf16[16,16,8,512]{3,2,1,0:T(8,128)(2,1)} %bitcast.8), channel_id=1, replica_groups=mesh['grp'=2,'stn'=4,'chan'=4] {'chan','stn'}, dimensions={0} | all-to-all | bytes 4194304 | tf_op jit(solution)/shard_map/all_to_all | solution.py:352
  75.9 7.8 %correlate.1 = bf16[4,3,16,16,128]{4,3,2,1,0:T(8,128)(2,1)} custom-call(bf16[16,16,8,512]{3,2,1,0:T(8,128)(2,1)} %all_to_all.10.r_ref), custom_call_target="tpu_custom_call" | custom-call | tf_op jit(solution)/shard_map/correlate/pallas_call | solution.py:326
  83.7 23.8 %all_to_all.11 = bf16[4,3,16,16,128]{4,3,2,1,0:T(8,128)(2,1)S(1)} all-to-all(bf16[4,3,16,16,128]{4,3,2,1,0:T(8,128)(2,1)} %correlate.1), channel_id=1, replica_groups=mesh['grp'=2,'stn'=4,'chan'=4] {'stn'}, dimensions={0} | all-to-all | bytes 1572864 | tf_op jit(solution)/shard_map/all_to_all | solution.py:354
  107.5 0.2 copy.6
  107.7 0.5 copy.9
  108.2 1.1 reshape.12
